TPU v7x, 128 devices: a whole 4x4x4 slice. The times are simulated.
128 devices in a mesh: slab: 32 (over y, z, core), col: 4 (over x).
Axes of the slice: x: 4, y: 4, z: 4, core: 2. Of those that a mesh axis runs over, the one named last changes fastest.
Arguments:
- input_map: float32 [64, 64, 192, 128], P('col', 'slab'), may hold values from -24 to 24
- output_map: float32 [64, 64, 192, 128], P('col', 'slab'), may hold values from -24 to 24
- region_ids: int32 [64, 192, 128], P('slab'), may hold values from 0 to 7
- region_cond: float32 [8], replicated, may hold values from 0.3 to 3
- shift_ids: int32 [2], replicated, may hold values from 0 to 7
Outputs:
- ctrl_factor: float32 [2, 64, 64, 192, 128], P(None, None, 'slab', 'col')
- obsv_factor: float32 [2, 64, 64, 192, 128], P(None, None, 'slab', 'col')
- cross_gram: float32 [128, 128], P('slab', 'col')
All inputs are finite; a program needn't handle non-finite values.
Results may differ from a plain program's by a relative error of at most 0.000098.
Values sent between devices are 32-bit elements; how exact they have to be, the bound alone decides.
A program may use at most 192 MiB of HBM per device.

v0:
```python
import math
import jax
import jax.numpy as jnp
from jax import lax
from jax.sharding import PartitionSpec as P

ADI = 2
STEPS = 3


def extended(block, sides, width):
    for axis, dim in sides:
        count = lax.axis_size(axis)
        forward = [(i, i + 1) for i in range(count - 1)]
        backward = [(target, source) for source, target in forward]
        low = lax.ppermute(
            lax.slice_in_dim(block, block.shape[dim] - width, None, axis=dim), axis, forward
        )
        high = lax.ppermute(lax.slice_in_dim(block, 0, width, axis=dim), axis, backward)
        block = jnp.concatenate([low, block, high], axis=dim)
    return block


def lookup(region_ids, region_cond):
    summed = jnp.zeros(region_ids.shape, jnp.float32)
    for region in range(region_cond.shape[0]):
        summed = summed + jnp.where(region_ids == region, region_cond[region], jnp.float32(0.0))
    return summed


def conduction(field_in, cond_ext):
    centre = field_in[:, 1:-1]
    cond_mid = cond_ext[1:-1]
    summed = 0.5 * (cond_mid + cond_ext[2:]) * (centre - field_in[:, 2:])
    summed = summed + 0.5 * (cond_mid + cond_ext[:-2]) * (centre - field_in[:, :-2])
    cond_y = jnp.pad(cond_mid, ((0, 0), (1, 1), (0, 0)))
    field_y = jnp.pad(centre, ((0, 0), (0, 0), (1, 1), (0, 0)))
    summed = summed + 0.5 * (cond_mid + cond_y[:, 2:]) * (centre - field_y[:, :, 2:])
    summed = summed + 0.5 * (cond_mid + cond_y[:, :-2]) * (centre - field_y[:, :, :-2])
    cond_z = jnp.pad(cond_mid, ((0, 0), (0, 0), (1, 1)))
    field_z = jnp.pad(centre, ((0, 0), (0, 0), (0, 0), (1, 1)))
    summed = summed + 0.5 * (cond_mid + cond_z[:, :, 2:]) * (centre - field_z[:, :, :, 2:])
    summed = summed + 0.5 * (cond_mid + cond_z[:, :, :-2]) * (centre - field_z[:, :, :, :-2])
    return summed


def bounds(shift_val, cond_max):
    high_eig = shift_val + 12.0 * cond_max
    mid_eig = 0.5 * (high_eig + shift_val)
    half_span = 0.5 * (high_eig - shift_val)
    return (mid_eig, half_span, mid_eig / half_span)


def solve_slabs(right_side, shift_val, cond_max, cond_ext):
    mid_eig, half_span, ratio_eig = bounds(shift_val, cond_max)
    rho_now = 1.0 / ratio_eig
    solution = jnp.zeros_like(right_side)
    residual = right_side
    direction = right_side / mid_eig
    for sweep_idx in range(STEPS - 1):
        solution = solution + direction
        padded = extended(direction, (("slab", 1),), 1)
        applied = conduction(padded, cond_ext) + shift_val * direction
        residual = residual - applied
        rho_next = 1.0 / (2.0 * ratio_eig - rho_now)
        direction = rho_next * rho_now * direction + 2.0 * rho_next / half_span * residual
        rho_now = rho_next
    return solution + direction


def run_segments(stacked, shifts, solver):
    factors = []
    current = stacked
    for segment_idx in range(ADI):
        shift_val = shifts[segment_idx]
        if segment_idx == 0:
            current = solver(stacked, shift_val)
        else:
            current = current - (shifts[segment_idx - 1] + shift_val) * solver(current, shift_val)
        factors.append(jnp.sqrt(2.0 * shift_val) * current)
    return jnp.stack(factors)


def body(input_map, output_map, region_ids, region_cond, shift_ids):
    col_local = input_map.shape[0]
    local_x = input_map.shape[1]
    cond_cells = lookup(region_ids, region_cond)
    cond_max = jnp.max(region_cond)
    shifts = 0.25 * jnp.exp2(shift_ids.astype(jnp.float32))
    total_x = local_x * lax.axis_size("slab")
    stacked = jnp.concatenate([input_map, output_map], 0)
    cond_ext = extended(cond_cells, (("slab", 0),), 1)
    factor_stack = run_segments(
        stacked, shifts, lambda rhs, shift_val: solve_slabs(rhs, shift_val, cond_max, cond_ext)
    )
    ctrl_local = factor_stack[:, :col_local]
    obsv_local = factor_stack[:, col_local:]
    ctrl_cols, obsv_cols = (
        lax.all_to_all(ctrl_local, "col", split_axis=3, concat_axis=1, tiled=True),
        lax.all_to_all(obsv_local, "col", split_axis=3, concat_axis=1, tiled=True),
    )
    row_count = ctrl_cols.shape[0] * ctrl_cols.shape[1]
    ctrl_flat = ctrl_cols.reshape(row_count, -1)
    obsv_flat = obsv_cols.reshape(row_count, -1)
    partial_value = lax.dot_general(
        ctrl_flat,
        obsv_flat,
        (((1,), (1,)), ((), ())),
        precision=lax.Precision.HIGHEST,
        preferred_element_type=jnp.float32,
    )
    cells_total = total_x * region_ids.shape[1] * region_ids.shape[2]
    norm_scale = 1.0 / math.sqrt(cells_total)
    whole_sum = lax.psum(partial_value, ("slab", "col"))
    tile_rows = row_count // lax.axis_size("slab")
    tile_cols = row_count // lax.axis_size("col")
    own_tile = lax.dynamic_slice(
        whole_sum,
        (lax.axis_index("slab") * tile_rows, lax.axis_index("col") * tile_cols),
        (tile_rows, tile_cols),
    )
    return (ctrl_cols, obsv_cols, own_tile * norm_scale)


def solution(mesh):
    placed = (
        P("col", "slab", None, None),
        P("col", "slab", None, None),
        P("slab", None, None),
        P(),
        P(),
    )
    return jax.shard_map(
        body,
        mesh=mesh,
        in_specs=placed,
        out_specs=(
            P(None, None, "slab", "col", None),
            P(None, None, "slab", "col", None),
            P("slab", "col"),
        ),
        check_vma=False,
    )
```

profile of v0, /device:TPU:1, one launch (start us, length us, event | category | flops | bytes accessed | tf_op | source)
XLA Modules:
  0.0 643.6 jit_solution(5252572299411760887)
XLA Ops:
  7.2 0.0 copy-start.5
  7.2 0.8 exponential_multiply_fusion
  8.0 0.6 fusion.108
  8.6 1.3 reduce_max.9
  11.8 3.9 constant_dynamic-update-slice_fusion.1
  15.7 0.0 copy-done.5
  15.7 1.9 constant_dynamic-update-slice_fusion
  17.6 3.2 broadcast_divide_fusion.1
  20.9 0.0 copy-start.1
  20.9 0.0 copy-start.7
  20.9 0.0 copy-start.6
  20.9 3.3 fusion.105
  24.2 1.3 copy-done.1
  25.4 3.3 collective-permute-start.1
  28.8 3.5 collective-permute-start.3
  32.3 0.0 copy-done.7
  32.3 0.7 fusion.107
  33.0 5.2 select_add_fusion
  38.2 2.5 collective-permute-start
  40.7 3.1 collective-permute-start.2
  44.6 22.0 %collective-permute-done = f32[1,192,128]{2,1,0:T(8,128)S(1)} collective-permute-done((f32[1,192,128]{2,1,0:T(8,128)S(1)}, f32[1,192,128]{2,1,0:T(8,128)S(1)}, u32[]{:S(2)}, u32[]{:S(2)}) %collective-permute-start) | collective-permute-done | bytes 98336 | tf_op jit(solution)/shard_map/ppermute | solution.py:19
  66.6 1.2 collective-permute-done.2
  67.8 0.2 fusion.98
  67.9 0.0 collective-permute-done.1
  68.0 0.0 collective-permute-done.3
  68.0 23.3 %multiply_add_fusion.1 = (f32[32,2,192,128]{3,2,1,0:T(8,128)S(1)}, f32[32,2,192,128]{3,2,1,0:T(8,128)}) fusion(f32[32,2,192,128]{3,2,1,0:T(8,128)} %copy-done.1, f32[]{:T(128)S(6)} %div.53, f32[]{:T(128)S(6)} %mul.354, f32[32,2,192,128]{3,2,1,0:T(8,128)} %constant_dynamic-update-slice_fusion, f32[]{:T(128)} %bitcast, ...), kind=kLoop, calls=%fused_computation.116 | loop fusion | flops 39321600 | bytes 32636940 | tf_op jit(solution)/shard_map/add | solution.py:66
  91.3 3.2 fusion.104
  94.6 1.4 copy-done.3
  95.9 1.9 collective-permute-start.4
  97.8 4.4 collective-permute-start.5
  103.6 32.0 %collective-permute-done.4 = f32[32,1,192,128]{3,2,1,0:T(8,128)} collective-permute-done((f32[32,1,192,128]{3,2,1,0:T(8,128)}, f32[32,1,192,128]{3,2,1,0:T(8,128)}, u32[]{:S(2)}, u32[]{:S(2)}) %collective-permute-start.4) | collective-permute-done | bytes 3145760 | tf_op jit(solution)/shard_map/ppermute | solution.py:19
  135.5 1.2 collective-permute-done.5
  136.7 26.0 %broadcast_divide_fusion = (f32[32,2,192,128]{3,2,1,0:T(8,128)S(1)}, f32[32,2,192,128]{3,2,1,0:T(8,128)}) fusion(f32[]{:T(128)S(6)} %mul.397, f32[32,2,192,128]{3,2,1,0:T(8,128)} %get-tuple-element.8, f32[32,2,192,128]{3,2,1,0:T(8,128)} %copy-done.3, f32[]{:T(128)} %bitcast, f32[2,192,128]{2,1,0:T(8,128)S(1)} %get-tuple-element.29, ...), kind=kLoop, calls=%fused_computation.117 | loop fusion | flops 45613056 | bytes 38928404 | tf_op jit(solution)/shard_map/div | solution.py:59
  162.7 3.8 fusion.103
  166.5 0.8 copy-done.2
  167.3 1.9 collective-permute-start.6
  169.2 4.4 collective-permute-start.7
  175.1 31.8 %collective-permute-done.6 = f32[32,1,192,128]{3,2,1,0:T(8,128)} collective-permute-done((f32[32,1,192,128]{3,2,1,0:T(8,128)}, f32[32,1,192,128]{3,2,1,0:T(8,128)}, u32[]{:S(2)}, u32[]{:S(2)}) %collective-permute-start.6) | collective-permute-done | bytes 3145760 | tf_op jit(solution)/shard_map/ppermute | solution.py:19
  207.0 1.2 collective-permute-done.7
  208.1 26.6 %multiply_add_fusion = (f32[32,2,192,128]{3,2,1,0:T(8,128)S(1)}, f32[32,2,192,128]{3,2,1,0:T(8,128)}, f32[1,32,2,192,128]{4,3,2,1,0:T(8,128)}) fusion(f32[]{:T(128)S(6)} %div.61, f32[]{:T(128)S(6)} %mul.400, f32[32,2,192,128]{3,2,1,0:T(8,128)} %get-tuple-element.6, f32[]{:T(128)S(6)} %mul.397, f32[32,2,192,128]{3,2,1,0:T(8,128)} %copy-done.2, f32[]{:T(128)} %bitcast.10, ...), kind=kLoop, calls=%fused_computation.114 | loop fusion | flops 42467328 | bytes 38928404 | tf_op jit(solution)/shard_map/add | solution.py:66
  234.7 0.0 copy-start
  234.7 3.8 fusion.102
  238.5 0.8 copy-done
  239.3 1.9 collective-permute-start.8
  241.2 4.6 collective-permute-start.9
  247.8 31.1 %collective-permute-done.8 = f32[32,1,192,128]{3,2,1,0:T(8,128)} collective-permute-done((f32[32,1,192,128]{3,2,1,0:T(8,128)}, f32[32,1,192,128]{3,2,1,0:T(8,128)}, u32[]{:S(2)}, u32[]{:S(2)}) %collective-permute-start.8) | collective-permute-done | bytes 3145760 | tf_op jit(solution)/shard_map/ppermute | solution.py:19
  278.9 1.2 collective-permute-done.9
  280.1 27.0 %fusion.47 = f32[1,32,2,192,128]{4,3,2,1,0:T(8,128)S(1)} fusion(f32[32,2,192,128]{3,2,1,0:T(8,128)} %get-tuple-element.6, f32[32,2,192,128]{3,2,1,0:T(8,128)} %get-tuple-element.4, f32[32,2,192,128]{3,2,1,0:T(8,128)} %copy-done, f32[32,1,192,128]{3,2,1,0:T(8,128)} %collective-permute-done.9, f32[32,1,192,128]{3,2,1,0:T(8,128)} %collective-permute-done.8, ...), kind=kLoop, calls=%fused_computation.65 | loop fusion | flops 48758784 | bytes 32636952 | tf_op jit(solution)/shard_map/stack | solution.py:81
  307.2 3.1 pad_maximum_fusion
  310.3 7.6 %copy.32 = f32[2,16,2,192,128]{4,2,1,0,3:T(2,128)} copy(f32[2,16,2,192,128]{4,3,2,1,0:T(8,128)S(1)} %get-tuple-element.10) | data formatting | bytes 12582912 | tf_op jit(solution)/shard_map/slice | solution.py:96
  317.9 5.3 all-to-all-start
  323.1 10.2 %copy.34 = f32[2,16,2,192,128]{4,2,1,0,3:T(2,128)} copy(f32[2,16,2,192,128]{4,3,2,1,0:T(8,128)} %get-tuple-element.9) | data formatting | bytes 12582912 | tf_op jit(solution)/shard_map/slice | solution.py:97
  333.4 51.1 %all-to-all-done = f32[2,16,2,192,128]{4,2,1,0,3:T(2,128)} async-done(((f32[2,16,2,192,128]{4,2,1,0,3:T(2,128)}), f32[2,16,2,192,128]{4,2,1,0,3:T(2,128)}, u32[]{:S(2)}, u32[]{:S(2)}) %all-to-all-start) | async-done | bytes 6291488 | tf_op jit(solution)/shard_map/all_to_all | solution.py:99
  384.5 5.2 all-to-all-start.1
  389.7 0.3 all-reduce.12.cloned.1.call-start
  390.0 9.0 %copy.41 = f32[2,16,2,4,48,128]{5,4,2,1,3,0:T(8,128)} copy(f32[2,16,2,4,48,128]{5,2,1,0,4,3:T(2,128)} %bitcast.12) | data formatting | bytes 12582912 | tf_op jit(solution)/shard_map/all_to_all | solution.py:99
  399.0 7.5 %reshape.20 = f32[128,12288]{1,0:T(8,128)} reshape(f32[2,4,16,2,48,128]{5,4,3,2,1,0:T(8,128)} %bitcast.32) | data formatting | bytes 12582912 | tf_op jit(solution)/shard_map/reshape | solution.py:103
  406.5 25.3 %all-to-all-done.1 = f32[2,16,2,192,128]{4,2,1,0,3:T(2,128)} async-done(((f32[2,16,2,192,128]{4,2,1,0,3:T(2,128)}), f32[2,16,2,192,128]{4,2,1,0,3:T(2,128)}, u32[]{:S(2)}, u32[]{:S(2)}) %all-to-all-start.1) | async-done | bytes 6291488 | tf_op jit(solution)/shard_map/all_to_all | solution.py:100
  431.7 9.0 %copy.40 = f32[2,16,2,4,48,128]{5,4,2,1,3,0:T(8,128)} copy(f32[2,16,2,4,48,128]{5,2,1,0,4,3:T(2,128)} %bitcast.15) | data formatting | bytes 12582912 | tf_op jit(solution)/shard_map/all_to_all | solution.py:100
  440.8 7.4 %reshape.21 = f32[128,12288]{1,0:T(8,128)} reshape(f32[2,4,16,2,48,128]{5,4,3,2,1,0:T(8,128)} %bitcast.34) | data formatting | bytes 12582912 | tf_op jit(solution)/shard_map/reshape | solution.py:104
  448.2 8.8 %fusion.109 = f32[128,128]{1,0:T(8,128)} fusion(f32[128,12288]{1,0:T(8,128)} %reshape.20, f32[128,12288]{1,0:T(8,128)} %reshape.21), kind=kOutput, calls=%fused_computation.151 | convolution fusion | flops 2415919104 | bytes 12648448 | tf_op jit(solution)/shard_map/dot_general | solution.py:105
  457.0 0.0 all-reduce.12.cloned.1.call-update
  457.1 178.4 %all-reduce.12.cloned.1.call-done = f32[128,128]{1,0:T(8,128)} async-done(((f32[128,128]{1,0:T(8,128)}), f32[128,128]{1,0:T(8,128)}) %all-reduce.12.cloned.1.call-update) | async-done | bytes 65552 | tf_op jit(solution)/shard_map/psum | solution.py:114
  635.4 1.3 dynamic-slice_multiply_fusion
  (6 shorter events, 0.0 us)
Async XLA Ops:
  7.2 8.6 %copy-start.5 = (f32[16,2,192,128]{3,2,1,0:T(8,128)S(1)}, f32[16,2,192,128]{3,2,1,0:T(8,128)}, u32[]{:S(2)}) copy-start(f32[16,2,192,128]{3,2,1,0:T(8,128)} %param.6) | copy-start | bytes 9437188
  20.9 4.6 copy-start.1
  20.9 11.4 %copy-start.7 = (f32[8]{0:T(128)S(1)}, f32[8]{0:T(128)}, u32[]{:S(2)}) copy-start(f32[8]{0:T(128)} %param.8) | copy-start | bytes 100
  20.9 12.1 %copy-start.6 = (s32[2,192,128]{2,1,0:T(8,128)S(1)}, s32[2,192,128]{2,1,0:T(8,128)}, u32[]{:S(2)}) copy-start(s32[2,192,128]{2,1,0:T(8,128)} %param.7) | copy-start | bytes 589828
  25.4 42.5 %collective-permute-start.1 = (f32[32,1,192,128]{3,2,1,0:T(8,128)}, f32[32,1,192,128]{3,2,1,0:T(8,128)}, u32[]{:S(2)}, u32[]{:S(2)}) collective-permute-start(f32[32,1,192,128]{3,2,1,0:T(8,128)} %get-tuple-element.22), channel_id=1, source_target_pairs={{4,0},{8,4},{12,8},{16,12},{20,16},{24,20},{28,24},{32,28},{36,32}... | collective-permute-start | bytes 9437192 | tf_op jit(solution)/shard_map/ppermute | solution.py:19
  28.8 39.2 %collective-permute-start.3 = (f32[32,1,192,128]{3,2,1,0:T(8,128)}, f32[32,1,192,128]{3,2,1,0:T(8,128)}, u32[]{:S(2)}, u32[]{:S(2)}) collective-permute-start(f32[32,1,192,128]{3,2,1,0:T(8,128)} %get-tuple-element.23), channel_id=1, source_target_pairs={{0,4},{4,8},{8,12},{12,16},{16,20},{20,24},{24,28},{28,32},{32,36}... | collective-permute-start | bytes 9437192 | tf_op jit(solution)/shard_map/ppermute | solution.py:16
  38.2 28.4 %collective-permute-start = (f32[1,192,128]{2,1,0:T(8,128)S(1)}, f32[1,192,128]{2,1,0:T(8,128)S(1)}, u32[]{:S(2)}, u32[]{:S(2)}) collective-permute-start(f32[1,192,128]{2,1,0:T(8,128)S(1)} %get-tuple-element.30), channel_id=1, source_target_pairs={{4,0},{8,4},{12,8},{16,12},{20,16},{24,20},{28,24},{32,28},{36,32}... | collective-permute-start | bytes 294920 | tf_op jit(solution)/shard_map/ppermute | solution.py:19
  40.7 27.1 %collective-permute-start.2 = (f32[1,192,128]{2,1,0:T(8,128)S(1)}, f32[1,192,128]{2,1,0:T(8,128)S(1)}, u32[]{:S(2)}, u32[]{:S(2)}) collective-permute-start(f32[1,192,128]{2,1,0:T(8,128)S(1)} %get-tuple-element.31), channel_id=1, source_target_pairs={{0,4},{4,8},{8,12},{12,16},{16,20},{20,24},{24,28},{28,32},{32,36}... | collective-permute-start | bytes 294920 | tf_op jit(solution)/shard_map/ppermute | solution.py:16
  91.3 4.6 copy-start.3
  95.9 39.6 %collective-permute-start.4 = (f32[32,1,192,128]{3,2,1,0:T(8,128)}, f32[32,1,192,128]{3,2,1,0:T(8,128)}, u32[]{:S(2)}, u32[]{:S(2)}) collective-permute-start(f32[32,1,192,128]{3,2,1,0:T(8,128)} %get-tuple-element.20), channel_id=1, source_target_pairs={{4,0},{8,4},{12,8},{16,12},{20,16},{24,20},{28,24},{32,28},{36,32}... | collective-permute-start | bytes 9437192 | tf_op jit(solution)/shard_map/ppermute | solution.py:19
  97.8 38.9 %collective-permute-start.5 = (f32[32,1,192,128]{3,2,1,0:T(8,128)}, f32[32,1,192,128]{3,2,1,0:T(8,128)}, u32[]{:S(2)}, u32[]{:S(2)}) collective-permute-start(f32[32,1,192,128]{3,2,1,0:T(8,128)} %get-tuple-element.21), channel_id=1, source_target_pairs={{0,4},{4,8},{8,12},{12,16},{16,20},{20,24},{24,28},{28,32},{32,36}... | collective-permute-start | bytes 9437192 | tf_op jit(solution)/shard_map/ppermute | solution.py:16
  162.7 4.6 copy-start.2
  167.3 39.6 %collective-permute-start.6 = (f32[32,1,192,128]{3,2,1,0:T(8,128)}, f32[32,1,192,128]{3,2,1,0:T(8,128)}, u32[]{:S(2)}, u32[]{:S(2)}) collective-permute-start(f32[32,1,192,128]{3,2,1,0:T(8,128)} %get-tuple-element.18), channel_id=1, source_target_pairs={{4,0},{8,4},{12,8},{16,12},{20,16},{24,20},{28,24},{32,28},{36,32}... | collective-permute-start | bytes 9437192 | tf_op jit(solution)/shard_map/ppermute | solution.py:19
  169.2 38.9 %collective-permute-start.7 = (f32[32,1,192,128]{3,2,1,0:T(8,128)}, f32[32,1,192,128]{3,2,1,0:T(8,128)}, u32[]{:S(2)}, u32[]{:S(2)}) collective-permute-start(f32[32,1,192,128]{3,2,1,0:T(8,128)} %get-tuple-element.19), channel_id=1, source_target_pairs={{0,4},{4,8},{8,12},{12,16},{16,20},{20,24},{24,28},{28,32},{32,36}... | collective-permute-start | bytes 9437192 | tf_op jit(solution)/shard_map/ppermute | solution.py:16
  234.7 4.6 copy-start
  239.3 39.6 %collective-permute-start.8 = (f32[32,1,192,128]{3,2,1,0:T(8,128)}, f32[32,1,192,128]{3,2,1,0:T(8,128)}, u32[]{:S(2)}, u32[]{:S(2)}) collective-permute-start(f32[32,1,192,128]{3,2,1,0:T(8,128)} %get-tuple-element.15), channel_id=1, source_target_pairs={{4,0},{8,4},{12,8},{16,12},{20,16},{24,20},{28,24},{32,28},{36,32}... | collective-permute-start | bytes 9437192 | tf_op jit(solution)/shard_map/ppermute | solution.py:19
  241.2 38.9 %collective-permute-start.9 = (f32[32,1,192,128]{3,2,1,0:T(8,128)}, f32[32,1,192,128]{3,2,1,0:T(8,128)}, u32[]{:S(2)}, u32[]{:S(2)}) collective-permute-start(f32[32,1,192,128]{3,2,1,0:T(8,128)} %get-tuple-element.16), channel_id=1, source_target_pairs={{0,4},{4,8},{8,12},{12,16},{16,20},{20,24},{24,28},{28,32},{32,36}... | collective-permute-start | bytes 9437192 | tf_op jit(solution)/shard_map/ppermute | solution.py:16
  280.1 27.0 %copy-start.4 = (f32[1,32,2,192,128]{4,3,2,1,0:T(8,128)S(1)}, f32[1,32,2,192,128]{4,3,2,1,0:T(8,128)}, u32[]{:S(2)}) copy-start(f32[1,32,2,192,128]{4,3,2,1,0:T(8,128)} %get-tuple-element.17) | copy-start | bytes 18874372
  317.9 66.6 %all-to-all-start = ((f32[2,16,2,192,128]{4,2,1,0,3:T(2,128)}), f32[2,16,2,192,128]{4,2,1,0,3:T(2,128)}, u32[]{:S(2)}, u32[]{:S(2)}) async-start(f32[2,16,2,192,128]{4,2,1,0,3:T(2,128)} %copy.32), calls=%async_computation | async-start | bytes 12582912 | tf_op jit(solution)/shard_map/all_to_all | solution.py:99
  384.5 47.3 %all-to-all-start.1 = ((f32[2,16,2,192,128]{4,2,1,0,3:T(2,128)}), f32[2,16,2,192,128]{4,2,1,0,3:T(2,128)}, u32[]{:S(2)}, u32[]{:S(2)}) async-start(f32[2,16,2,192,128]{4,2,1,0,3:T(2,128)} %copy.34), calls=%async_computation.1 | async-start | bytes 12582912 | tf_op jit(solution)/shard_map/all_to_all | solution.py:100
  389.7 245.7 %all-reduce.12.cloned.1.call-start = ((), (), s32[]{:S(2)}) async-start(), calls=%async_computation.2 | async-start | bytes 131072 | tf_op jit(solution)/shard_map/psum | solution.py:114
Sparse Core Ops, SparseCore 0:
  457.2 178.1 all-reduce.11
where the time goes:
time: 645 us; the launch traced here: 644 us
  waiting for transfers between devices  376 us (58%)
  other arithmetic  118 us (18%)
  local copies, waits for them, and re-layouts  76.2 us (12%)
  starting transfers between devices  42.3 us (7%)
  between operations  21.9 us (3%)
  matrix products  8.8 us (1%)
    psum x1, waiting for transfers between devices, body(): whole_sum = lax.psum(partial_value, ('slab', 'col'))  178 us
    ppermute x5, waiting for transfers between devices, extended(): lax.ppermute(lax.slice_in_dim(block, 0, width, axis=dim), axis, backward)  117 us
    all_to_all x1, waiting for transfers between devices, body(): lax.all_to_all(ctrl_local, 'col', split_axis=3, concat_axis=1, tiled=True)  51.1 us
    add x2, other arithmetic, solve_slabs(): rho_next * rho_now * direction + 2.0 * rho_next / half_span * residual  49.9 us
    another operation x2, other arithmetic, run_segments(): return jnp.stack(factors)  30.2 us
    div x2, other arithmetic, solve_slabs(): direction = right_side / mid_eig  29.2 us
    all_to_all x1, waiting for transfers between devices, body(): lax.all_to_all(obsv_local, 'col', split_axis=3, concat_axis=1, tiled=True)  25.3 us
    ppermute x5, starting transfers between devices, extended(): lax.ppermute(lax.slice_in_dim(block, block.shape[dim] - width, None, axis...  19.9 us
  transfers between devices with their start and end apart: 13, of which 11 were waited for; matrix products, arithmetic and copies ran while one was open for 5% of the time, Pallas kernels for 0%

commit v1 on v0

--- a/solution.py
+++ b/solution.py
@@ -95,9 +95,31 @@
     )
     ctrl_local = factor_stack[:, :col_local]
     obsv_local = factor_stack[:, col_local:]
+
+    def _solve_cards(dim_i, d_out, u_in):
+        known, base_arr = (lax.axis_size("col"), lax.axis_index("col"))
+        finding = u_in.shape[dim_i] // known
+        moved = list(u_in.shape)
+        moved[dim_i] = finding
+        work_now = moved[d_out]
+        moved[d_out] = work_now * known
+        t = 0
+        back = jnp.zeros(moved, u_in.dtype)
+        while t < known:
+            vec_out = lax.dynamic_slice_in_dim(u_in, (base_arr ^ t) * finding, finding, axis=dim_i)
+            if t:
+                vec_out = lax.ppermute(
+                    vec_out, axis_name="col", perm=[(num, num ^ t) for num in range(known)]
+                )
+            back = lax.dynamic_update_slice_in_dim(
+                back, vec_out, (base_arr ^ t) * work_now, axis=d_out
+            )
+            t = t + 1
+        return back
+
     ctrl_cols, obsv_cols = (
         lax.all_to_all(ctrl_local, "col", split_axis=3, concat_axis=1, tiled=True),
-        lax.all_to_all(obsv_local, "col", split_axis=3, concat_axis=1, tiled=True),
+        _solve_cards(3, 1, obsv_local),
     )
     row_count = ctrl_cols.shape[0] * ctrl_cols.shape[1]
     ctrl_flat = ctrl_cols.reshape(row_count, -1)

time: 645 us -> 651 us (level)
  waiting for transfers between devices: 376 us -> 389 us
    ppermute x0 -> x3, waiting for transfers between devices: none -> 92.9 us  [_solve_cards(): lax.ppermute(vec_out, axis_name='col', perm=[(num, num ^ t) for num in ra...]
    all_to_all x1, waiting for transfers between devices: 51.1 us -> 0.01 us  [body(): lax.all_to_all(ctrl_local, 'col', split_axis=3, concat_axis=1, tiled=True)]
    all_to_all x1 -> x0, waiting for transfers between devices: 25.3 us -> none  [body(): lax.all_to_all(obsv_local, 'col', split_axis=3, concat_axis=1, tiled=True)]
    slice x2 -> x0, local copies, waits for them, and re-layouts: 17.8 us -> none  [the longest x1 10.2 us: body(): obsv_local = factor_stack[:, col_local:]]
    unnamed x17 -> x26, local copies, waits for them, and re-layouts: 8.16 us -> 22 us
    all_to_all x1 -> x0, local copies, waits for them, and re-layouts: 9.04 us -> none  [body(): lax.all_to_all(obsv_local, 'col', split_axis=3, concat_axis=1, tiled=True)]
    dynamic_update_slice x0 -> x3, local copies, waits for them, and re-layouts: none -> 7.97 us  [_solve_cards(): lax.dynamic_update_slice_in_dim(back, vec_out, (base_arr ^ t) * work_now,...]
    another operation x2 -> x3, other arithmetic: 30.2 us -> 31 us  [run_segments(): return jnp.stack(factors)]
  transfers between devices with their start and end apart: 13 -> 15, of which waited for: 11 -> 11; matrix products, arithmetic and copies ran while one was open for 5% -> 4% of each run, Pallas kernels for 0% -> 0%
where the time goes in v1:
time: 651 us; the launch traced here: 650 us
  waiting for transfers between devices  389 us (60%)
  other arithmetic  119 us (18%)
  local copies, waits for them, and re-layouts  71.5 us (11%)
  starting transfers between devices  40.6 us (6%)
  between operations  21.6 us (3%)
  matrix products  8.81 us (1%)
    psum x1, waiting for transfers between devices, body(): whole_sum = lax.psum(partial_value, ('slab', 'col'))  174 us
    ppermute x5, waiting for transfers between devices, extended(): lax.ppermute(lax.slice_in_dim(block, 0, width, axis=dim), axis, backward)  117 us
    ppermute x3, waiting for transfers between devices, _solve_cards(): lax.ppermute(vec_out, axis_name='col', perm=[(num, num ^ t) for num in ra...  92.9 us
    add x2, other arithmetic, solve_slabs(): rho_next * rho_now * direction + 2.0 * rho_next / half_span * residual  49.8 us
    another operation x3, other arithmetic, run_segments(): return jnp.stack(factors)  31 us
    div x2, other arithmetic, solve_slabs(): direction = right_side / mid_eig  29.1 us
    unnamed x26, local copies, waits for them, and re-layouts  22 us
    ppermute x5, starting transfers between devices, extended(): lax.ppermute(lax.slice_in_dim(block, block.shape[dim] - width, None, axis...  19.9 us
  transfers between devices with their start and end apart: 15, of which 11 were waited for; matrix products, arithmetic and copies ran while one was open for 4% of the time, Pallas kernels for 0%

profile of v1, /device:TPU:1, one launch (start us, length us, event | category | flops | bytes accessed | tf_op | source)
XLA Modules:
  0.0 649.9 jit_solution(6869410976651268178)
XLA Ops:
  7.2 0.8 exponential_multiply_fusion
  8.0 0.6 fusion.113
  8.6 1.3 reduce_max.9
  11.8 3.9 constant_dynamic-update-slice_fusion.1
  15.7 1.9 constant_dynamic-update-slice_fusion
  17.6 3.2 broadcast_divide_fusion.1
  20.8 0.0 copy-start.3
  20.8 3.3 fusion.110
  24.1 1.3 copy-done.3
  25.4 3.3 collective-permute-start.1
  28.7 3.5 collective-permute-start.3
  32.3 0.7 fusion.112
  32.9 5.1 select_add_fusion
  38.0 2.5 collective-permute-start
  40.5 3.1 collective-permute-start.2
  44.4 22.1 %collective-permute-done = f32[1,192,128]{2,1,0:T(8,128)S(1)} collective-permute-done((f32[1,192,128]{2,1,0:T(8,128)S(1)}, f32[1,192,128]{2,1,0:T(8,128)S(1)}, u32[]{:S(2)}, u32[]{:S(2)}) %collective-permute-start) | collective-permute-done | bytes 98336 | tf_op jit(solution)/shard_map/ppermute | solution.py:19
  66.5 1.2 collective-permute-done.2
  67.7 0.2 fusion.103
  67.9 23.3 %multiply_add_fusion.1 = (f32[32,2,192,128]{3,2,1,0:T(8,128)S(1)}, f32[32,2,192,128]{3,2,1,0:T(8,128)}) fusion(f32[32,2,192,128]{3,2,1,0:T(8,128)} %copy-done.3, f32[]{:T(128)S(6)} %div.53, f32[]{:T(128)S(6)} %mul.378, f32[32,2,192,128]{3,2,1,0:T(8,128)} %constant_dynamic-update-slice_fusion, f32[]{:T(128)} %bitcast, ...), kind=kLoop, calls=%fused_computation.115 | loop fusion | flops 39321600 | bytes 32636940 | tf_op jit(solution)/shard_map/add | solution.py:66
  91.2 3.3 fusion.109
  94.5 1.3 copy-done.5
  95.8 1.9 collective-permute-start.4
  97.8 4.4 collective-permute-start.5
  103.4 32.1 %collective-permute-done.4 = f32[32,1,192,128]{3,2,1,0:T(8,128)} collective-permute-done((f32[32,1,192,128]{3,2,1,0:T(8,128)}, f32[32,1,192,128]{3,2,1,0:T(8,128)}, u32[]{:S(2)}, u32[]{:S(2)}) %collective-permute-start.4) | collective-permute-done | bytes 3145760 | tf_op jit(solution)/shard_map/ppermute | solution.py:19
  135.5 1.2 collective-permute-done.5
  136.7 25.9 %broadcast_divide_fusion = (f32[32,2,192,128]{3,2,1,0:T(8,128)S(1)}, f32[32,2,192,128]{3,2,1,0:T(8,128)}) fusion(f32[]{:T(128)S(6)} %mul.421, f32[32,2,192,128]{3,2,1,0:T(8,128)} %get-tuple-element.8, f32[32,2,192,128]{3,2,1,0:T(8,128)} %copy-done.5, f32[]{:T(128)} %bitcast, f32[2,192,128]{2,1,0:T(8,128)S(1)} %get-tuple-element.29, ...), kind=kLoop, calls=%fused_computation.124 | loop fusion | flops 45613056 | bytes 38928404 | tf_op jit(solution)/shard_map/div | solution.py:59
  162.5 3.8 fusion.108
  166.3 0.8 copy-done.4
  167.1 1.9 collective-permute-start.6
  169.1 4.4 collective-permute-start.7
  174.9 31.9 %collective-permute-done.6 = f32[32,1,192,128]{3,2,1,0:T(8,128)} collective-permute-done((f32[32,1,192,128]{3,2,1,0:T(8,128)}, f32[32,1,192,128]{3,2,1,0:T(8,128)}, u32[]{:S(2)}, u32[]{:S(2)}) %collective-permute-start.6) | collective-permute-done | bytes 3145760 | tf_op jit(solution)/shard_map/ppermute | solution.py:19
  206.8 1.2 collective-permute-done.7
  208.0 26.5 %multiply_add_fusion = (f32[32,2,192,128]{3,2,1,0:T(8,128)S(1)}, f32[32,2,192,128]{3,2,1,0:T(8,128)}, f32[1,32,2,192,128]{4,3,2,1,0:T(8,128)}) fusion(f32[]{:T(128)S(6)} %div.61, f32[]{:T(128)S(6)} %mul.424, f32[32,2,192,128]{3,2,1,0:T(8,128)} %get-tuple-element.6, f32[]{:T(128)S(6)} %mul.421, f32[32,2,192,128]{3,2,1,0:T(8,128)} %copy-done.4, f32[]{:T(128)} %bitcast.10, ...), kind=kLoop, calls=%fused_computation.113 | loop fusion | flops 42467328 | bytes 38928404 | tf_op jit(solution)/shard_map/add | solution.py:66
  234.5 3.4 fusion.107
  237.9 1.3 copy-done.2
  239.2 1.9 collective-permute-start.8
  241.1 4.6 collective-permute-start.9
  247.6 31.3 %collective-permute-done.8 = f32[32,1,192,128]{3,2,1,0:T(8,128)} collective-permute-done((f32[32,1,192,128]{3,2,1,0:T(8,128)}, f32[32,1,192,128]{3,2,1,0:T(8,128)}, u32[]{:S(2)}, u32[]{:S(2)}) %collective-permute-start.8) | collective-permute-done | bytes 3145760 | tf_op jit(solution)/shard_map/ppermute | solution.py:19
  278.9 1.2 collective-permute-done.9
  280.0 26.9 %fusion.47 = f32[1,32,2,192,128]{4,3,2,1,0:T(8,128)S(1)} fusion(f32[32,2,192,128]{3,2,1,0:T(8,128)} %get-tuple-element.6, f32[32,2,192,128]{3,2,1,0:T(8,128)} %get-tuple-element.4, f32[32,2,192,128]{3,2,1,0:T(8,128)} %copy-done.2, f32[32,1,192,128]{3,2,1,0:T(8,128)} %collective-permute-done.9, f32[32,1,192,128]{3,2,1,0:T(8,128)} %collective-permute-done.8, ...), kind=kLoop, calls=%fused_computation.65 | loop fusion | flops 48758784 | bytes 32636952 | tf_op jit(solution)/shard_map/stack | solution.py:81
  307.0 0.4 fusion.50
  307.4 2.2 copy-done
  309.7 6.3 copy.26
  316.0 5.3 all-to-all-start
  321.3 0.0 all-reduce.12.cloned.1.call-start
  321.4 0.8 broadcast_in_dim.72
  322.2 2.0 copy-done.1
  324.1 3.7 fusion.87
  327.8 2.7 copy-done.6
  330.5 1.3 collective-permute-start.10
  331.9 2.4 collective-permute-start.11
  334.3 0.1 collective-permute-start.12
  334.4 77.2 %collective-permute-done.10 = f32[2,16,2,48,128]{4,3,2,1,0:T(8,128)} collective-permute-done((f32[2,16,2,48,128]{4,3,2,1,0:T(8,128)}, f32[2,16,2,48,128]{4,3,2,1,0:T(8,128)}, u32[]{:S(2)}, u32[]{:S(2)}) %collective-permute-start.10) | collective-permute-done | bytes 1572896 | tf_op jit(solution)/shard_map/ppermute | solution.py:111
  411.6 2.7 constant_dynamic-update-slice_fusion.4
  414.3 15.7 %collective-permute-done.11 = f32[2,16,2,48,128]{4,3,2,1,0:T(8,128)} collective-permute-done((f32[2,16,2,48,128]{4,3,2,1,0:T(8,128)S(1)}, f32[2,16,2,48,128]{4,3,2,1,0:T(8,128)}, u32[]{:S(2)}, u32[]{:S(2)}) %collective-permute-start.11) | collective-permute-done | bytes 1572896 | tf_op jit(solution)/shard_map/ppermute | solution.py:111
  430.0 2.7 constant_dynamic-update-slice_fusion.3
  432.6 2.7 constant_dynamic-update-slice_fusion.2
  435.3 7.5 %reshape.20 = f32[128,12288]{1,0:T(8,128)} reshape(f32[2,64,2,48,128]{4,3,2,1,0:T(8,128)} %constant_dynamic-update-slice_fusion.2) | data formatting | bytes 12582912 | tf_op jit(solution)/shard_map/reshape | solution.py:126
  442.8 9.0 %copy.29 = f32[2,16,2,4,48,128]{5,4,2,1,3,0:T(8,128)} copy(f32[2,16,2,4,48,128]{5,1,2,0,4,3:T(8,128)} %bitcast.12) | data formatting | bytes 12582912 | tf_op jit(solution)/shard_map/all_to_all | solution.py:121
  451.8 7.4 %reshape.19 = f32[128,12288]{1,0:T(8,128)} reshape(f32[2,4,16,2,48,128]{5,4,3,2,1,0:T(8,128)} %bitcast.28) | data formatting | bytes 12582912 | tf_op jit(solution)/shard_map/reshape | solution.py:125
  459.2 8.8 %fusion.114 = f32[128,128]{1,0:T(8,128)} fusion(f32[128,12288]{1,0:T(8,128)} %reshape.19, f32[128,12288]{1,0:T(8,128)} %reshape.20), kind=kOutput, calls=%fused_computation.165 | convolution fusion | flops 2415919104 | bytes 12648448 | tf_op jit(solution)/shard_map/dot_general | solution.py:127
  468.1 0.0 all-reduce.12.cloned.1.call-update
  468.1 173.6 %all-reduce.12.cloned.1.call-done = f32[128,128]{1,0:T(8,128)} async-done(((f32[128,128]{1,0:T(8,128)}), f32[128,128]{1,0:T(8,128)}) %all-reduce.12.cloned.1.call-update) | async-done | bytes 65552 | tf_op jit(solution)/shard_map/psum | solution.py:136
  641.7 1.3 dynamic-slice_multiply_fusion
  (22 shorter events, 0.1 us)
Async XLA Ops:
  7.2 8.5 %copy-start.7 = (f32[16,2,192,128]{3,2,1,0:T(8,128)S(1)}, f32[16,2,192,128]{3,2,1,0:T(8,128)}, u32[]{:S(2)}) copy-start(f32[16,2,192,128]{3,2,1,0:T(8,128)} %param.6) | copy-start | bytes 9437188
  20.8 4.6 copy-start.3
  20.8 11.4 %copy-start.9 = (f32[8]{0:T(128)S(1)}, f32[8]{0:T(128)}, u32[]{:S(2)}) copy-start(f32[8]{0:T(128)} %param.8) | copy-start | bytes 100
  20.8 12.1 %copy-start.8 = (s32[2,192,128]{2,1,0:T(8,128)S(1)}, s32[2,192,128]{2,1,0:T(8,128)}, u32[]{:S(2)}) copy-start(s32[2,192,128]{2,1,0:T(8,128)} %param.7) | copy-start | bytes 589828
  25.4 42.5 %collective-permute-start.1 = (f32[32,1,192,128]{3,2,1,0:T(8,128)}, f32[32,1,192,128]{3,2,1,0:T(8,128)}, u32[]{:S(2)}, u32[]{:S(2)}) collective-permute-start(f32[32,1,192,128]{3,2,1,0:T(8,128)} %get-tuple-element.22), channel_id=1, source_target_pairs={{4,0},{8,4},{12,8},{16,12},{20,16},{24,20},{28,24},{32,28},{36,32}... | collective-permute-start | bytes 9437192 | tf_op jit(solution)/shard_map/ppermute | solution.py:19
  28.7 39.2 %collective-permute-start.3 = (f32[32,1,192,128]{3,2,1,0:T(8,128)}, f32[32,1,192,128]{3,2,1,0:T(8,128)}, u32[]{:S(2)}, u32[]{:S(2)}) collective-permute-start(f32[32,1,192,128]{3,2,1,0:T(8,128)} %get-tuple-element.23), channel_id=1, source_target_pairs={{0,4},{4,8},{8,12},{12,16},{16,20},{20,24},{24,28},{28,32},{32,36}... | collective-permute-start | bytes 9437192 | tf_op jit(solution)/shard_map/ppermute | solution.py:16
  38.0 28.5 %collective-permute-start = (f32[1,192,128]{2,1,0:T(8,128)S(1)}, f32[1,192,128]{2,1,0:T(8,128)S(1)}, u32[]{:S(2)}, u32[]{:S(2)}) collective-permute-start(f32[1,192,128]{2,1,0:T(8,128)S(1)} %get-tuple-element.30), channel_id=1, source_target_pairs={{4,0},{8,4},{12,8},{16,12},{20,16},{24,20},{28,24},{32,28},{36,32}... | collective-permute-start | bytes 294920 | tf_op jit(solution)/shard_map/ppermute | solution.py:19
  40.5 27.2 %collective-permute-start.2 = (f32[1,192,128]{2,1,0:T(8,128)S(1)}, f32[1,192,128]{2,1,0:T(8,128)S(1)}, u32[]{:S(2)}, u32[]{:S(2)}) collective-permute-start(f32[1,192,128]{2,1,0:T(8,128)S(1)} %get-tuple-element.31), channel_id=1, source_target_pairs={{0,4},{4,8},{8,12},{12,16},{16,20},{20,24},{24,28},{28,32},{32,36}... | collective-permute-start | bytes 294920 | tf_op jit(solution)/shard_map/ppermute | solution.py:16
  91.2 4.6 copy-start.5
  95.8 39.6 %collective-permute-start.4 = (f32[32,1,192,128]{3,2,1,0:T(8,128)}, f32[32,1,192,128]{3,2,1,0:T(8,128)}, u32[]{:S(2)}, u32[]{:S(2)}) collective-permute-start(f32[32,1,192,128]{3,2,1,0:T(8,128)} %get-tuple-element.20), channel_id=1, source_target_pairs={{4,0},{8,4},{12,8},{16,12},{20,16},{24,20},{28,24},{32,28},{36,32}... | collective-permute-start | bytes 9437192 | tf_op jit(solution)/shard_map/ppermute | solution.py:19
  97.8 38.9 %collective-permute-start.5 = (f32[32,1,192,128]{3,2,1,0:T(8,128)}, f32[32,1,192,128]{3,2,1,0:T(8,128)}, u32[]{:S(2)}, u32[]{:S(2)}) collective-permute-start(f32[32,1,192,128]{3,2,1,0:T(8,128)} %get-tuple-element.21), channel_id=1, source_target_pairs={{0,4},{4,8},{8,12},{12,16},{16,20},{20,24},{24,28},{28,32},{32,36}... | collective-permute-start | bytes 9437192 | tf_op jit(solution)/shard_map/ppermute | solution.py:16
  162.5 4.6 copy-start.4
  167.1 39.6 %collective-permute-start.6 = (f32[32,1,192,128]{3,2,1,0:T(8,128)}, f32[32,1,192,128]{3,2,1,0:T(8,128)}, u32[]{:S(2)}, u32[]{:S(2)}) collective-permute-start(f32[32,1,192,128]{3,2,1,0:T(8,128)} %get-tuple-element.18), channel_id=1, source_target_pairs={{4,0},{8,4},{12,8},{16,12},{20,16},{24,20},{28,24},{32,28},{36,32}... | collective-permute-start | bytes 9437192 | tf_op jit(solution)/shard_map/ppermute | solution.py:19
  169.1 38.9 %collective-permute-start.7 = (f32[32,1,192,128]{3,2,1,0:T(8,128)}, f32[32,1,192,128]{3,2,1,0:T(8,128)}, u32[]{:S(2)}, u32[]{:S(2)}) collective-permute-start(f32[32,1,192,128]{3,2,1,0:T(8,128)} %get-tuple-element.19), channel_id=1, source_target_pairs={{0,4},{4,8},{8,12},{12,16},{16,20},{20,24},{24,28},{28,32},{32,36}... | collective-permute-start | bytes 9437192 | tf_op jit(solution)/shard_map/ppermute | solution.py:16
  234.5 4.7 copy-start.2
  234.5 72.5 %slice-start = ((s8[6291456]{0:T(1024)(128)(4,1)}), s8[2097152]{0:T(1024)(128)(4,1)S(1)}, s32[]{:S(2)}) async-start(s8[6291456]{0:T(1024)(128)(4,1)} %bitcast.26), calls=%async_computation.2 | async-start | bytes 4194304
  239.2 39.6 %collective-permute-start.8 = (f32[32,1,192,128]{3,2,1,0:T(8,128)}, f32[32,1,192,128]{3,2,1,0:T(8,128)}, u32[]{:S(2)}, u32[]{:S(2)}) collective-permute-start(f32[32,1,192,128]{3,2,1,0:T(8,128)} %get-tuple-element.15), channel_id=1, source_target_pairs={{4,0},{8,4},{12,8},{16,12},{20,16},{24,20},{28,24},{32,28},{36,32}... | collective-permute-start | bytes 9437192 | tf_op jit(solution)/shard_map/ppermute | solution.py:19
  241.1 38.9 %collective-permute-start.9 = (f32[32,1,192,128]{3,2,1,0:T(8,128)}, f32[32,1,192,128]{3,2,1,0:T(8,128)}, u32[]{:S(2)}, u32[]{:S(2)}) collective-permute-start(f32[32,1,192,128]{3,2,1,0:T(8,128)} %get-tuple-element.16), channel_id=1, source_target_pairs={{0,4},{4,8},{8,12},{12,16},{16,20},{20,24},{24,28},{28,32},{32,36}... | collective-permute-start | bytes 9437192 | tf_op jit(solution)/shard_map/ppermute | solution.py:16
  280.0 27.0 %slice-start.1 = ((s8[6291456]{0:T(1024)(128)(4,1)}), s8[4194304]{0:T(1024)(128)(4,1)S(1)}, s32[]{:S(2)}) async-start(s8[6291456]{0:T(1024)(128)(4,1)} %bitcast.26), calls=%async_computation.3 | async-start | bytes 8388608
  307.0 2.7 copy-start
  316.0 126.7 %all-to-all-start = ((f32[2,16,2,192,128]{4,1,2,0,3:T(8,128)}), f32[2,16,2,192,128]{4,1,2,0,3:T(8,128)}, u32[]{:S(2)}, u32[]{:S(2)}) async-start(f32[2,16,2,192,128]{4,1,2,0,3:T(8,128)} %copy.26), calls=%async_computation | async-start | bytes 12582912 | tf_op jit(solution)/shard_map/all_to_all | solution.py:121
  321.3 320.4 %all-reduce.12.cloned.1.call-start = ((), (), s32[]{:S(2)}) async-start(), calls=%async_computation.1 | async-start | bytes 131072 | tf_op jit(solution)/shard_map/psum | solution.py:136
  321.4 2.8 copy-start.1
  327.8 2.7 copy-start.6
  330.5 81.1 %collective-permute-start.10 = (f32[2,16,2,48,128]{4,3,2,1,0:T(8,128)}, f32[2,16,2,48,128]{4,3,2,1,0:T(8,128)}, u32[]{:S(2)}, u32[]{:S(2)}) collective-permute-start(f32[2,16,2,48,128]{4,3,2,1,0:T(8,128)} %get-tuple-element.11), channel_id=1, source_target_pairs={{0,1},{1,0},{2,3},{3,2},{4,5},{5,4},{6,7},{7,6},{8,9},{9,8},{10,11... | collective-permute-start | bytes 4718600 | tf_op jit(solution)/shard_map/ppermute | solution.py:111
  331.9 98.1 %collective-permute-start.11 = (f32[2,16,2,48,128]{4,3,2,1,0:T(8,128)S(1)}, f32[2,16,2,48,128]{4,3,2,1,0:T(8,128)}, u32[]{:S(2)}, u32[]{:S(2)}) collective-permute-start(f32[2,16,2,48,128]{4,3,2,1,0:T(8,128)S(1)} %get-tuple-element.12), channel_id=1, source_target_pairs={{0,2},{1,3},{2,0},{3,1},{4,6},{5,7},{6,4},{7,5},{8,10},{9,11},{10,... | collective-permute-start | bytes 4718600 | tf_op jit(solution)/shard_map/ppermute | solution.py:111
  334.3 98.4 %collective-permute-start.12 = (f32[2,16,2,48,128]{4,3,2,1,0:T(8,128)S(1)}, f32[2,16,2,48,128]{4,3,2,1,0:T(8,128)}, u32[]{:S(2)}, u32[]{:S(2)}) collective-permute-start(f32[2,16,2,48,128]{4,3,2,1,0:T(8,128)S(1)} %get-tuple-element.9), channel_id=1, source_target_pairs={{0,3},{1,2},{2,1},{3,0},{4,7},{5,6},{6,5},{7,4},{8,11},{9,10},{10,... | collective-permute-start | bytes 4718600 | tf_op jit(solution)/shard_map/ppermute | solution.py:111
Sparse Core Ops, SparseCore 0:
  468.2 173.4 all-reduce.11
